TPU v7x, 256 devices: a whole 4x4x8 slice. The times are simulated.
256 devices in a mesh: row: 32 (over x, y, core), col: 8 (over z).
Axes of the slice: x: 4, y: 4, z: 8, core: 2. Of those that a mesh axis runs over, the one named last changes fastest.
Arguments:
- blocks: float32 [32, 8, 8, 32, 2, 8, 128], P('row', 'col'), may hold values from 0.5 to 1620
- plan: int32 [32, 8, 8, 32, 2], P('row', 'col'), may hold values from 0 to 4095, as said below
- live: int32 [32, 8, 8, 32], P('row', 'col'), may hold values from 1 to 2, as said below
- row_emb: float32 [300, 32768], P(None, ('row', 'col')), may hold values from -1.5 to 1.5
- col_emb: float32 [300, 32768], P(None, ('col', 'row')), may hold values from -1.5 to 1.5
- row_acc: float32 [300, 32768], P(None, ('row', 'col')), may hold values from 0.5 to 5
- col_acc: float32 [300, 32768], P(None, ('col', 'row')), may hold values from 0.5 to 5
Outputs:
- new_row_emb: float32 [300, 32768], P(None, ('row', 'col'))
- new_col_emb: float32 [300, 32768], P(None, ('col', 'row'))
- new_row_acc: float32 [300, 32768], P(None, ('row', 'col'))
- new_col_acc: float32 [300, 32768], P(None, ('col', 'row'))
Inputs may be any that keep to these rules, and one draw needn't show every extreme that they name: plan[r, c, c2, r2, p] is a sub-block number of tile (r, c); numbers may repeat and repeated slots add. Over all index pairs (r2, c2), slot 0 names every sub-block row and every sub-block column of each tile. Slots at or past live[r, c, c2, r2] hold values that are not counts. In every draw some tile gets 2 live slots from every index pair.
All inputs are finite; a program needn't handle non-finite values.
Results may differ from a plain program's by a relative error of at most 0.0003.
Values sent between devices are 32-bit elements; how exact they have to be, the bound alone decides.
No kernel may reach another device: no remote copies, remote signals or barrier semaphores. Data moves between devices by JAX's collectives and lax.ppermute only.
A program may use at most 192 MiB of HBM per device.

v0:
```python
import jax
import jax.numpy as jnp
from jax import lax
from jax.sharding import PartitionSpec as P

LEARNING_RATE = 0.2


def per_device(blocks, plan, live, row_emb, col_emb, row_acc, col_acc):
    rows_count = lax.axis_size("row")
    cols_count = lax.axis_size("col")
    highest = lax.Precision.HIGHEST
    outgoing = blocks[0, 0]
    arrived = lax.all_to_all(
        lax.all_to_all(outgoing, "row", split_axis=1, concat_axis=1, tiled=True),
        "col",
        split_axis=0,
        concat_axis=0,
        tiled=True,
    )
    sub_rows = blocks.shape[5]
    sub_cols = blocks.shape[6]
    tile_rows = row_emb.shape[1] * cols_count
    tile_cols = col_emb.shape[1] * rows_count
    grid_row_count = tile_rows // sub_rows
    grid_column_count = tile_cols // sub_cols
    block_total = grid_row_count * grid_column_count
    places = plan[0, 0]
    limits = live[0, 0]
    slot_ids = lax.broadcasted_iota(jnp.int32, places.shape, 2)
    target = jnp.where(slot_ids < limits[:, :, None], places, block_total)
    flat_layout = arrived.reshape(-1, sub_rows * sub_cols)
    dense_block_matrix = jax.ops.segment_sum(
        flat_layout, target.reshape(-1), num_segments=block_total + 1
    )[:block_total]
    tile_counts = (
        dense_block_matrix.reshape(grid_row_count, grid_column_count, sub_rows, sub_cols)
        .transpose(0, 2, 1, 3)
        .reshape(tile_rows, tile_cols)
    )
    row_part = jnp.sum(tile_counts, axis=1)
    col_part = jnp.sum(tile_counts, axis=0)
    col_mass = lax.psum(col_part, "row")
    row_mass = lax.psum(row_part, "col")
    grand_total = lax.psum(jnp.sum(row_part), ("row", "col"))
    row_block = lax.all_gather(row_emb, "col", axis=1, tiled=True)
    col_block = lax.all_gather(col_emb, "row", axis=1, tiled=True)
    rows_all = tile_rows * rows_count
    cols_all = tile_cols * cols_count
    loss_scale = 4.0 * float(rows_all * cols_all) ** (-0.25)
    col_base = jnp.log(grand_total) - jnp.log(col_mass)[None, :]
    row_logs = jnp.log(row_mass)
    step_rows = min(512, tile_rows)
    col_term = jnp.zeros((col_block.shape[0], tile_cols), jnp.float32)
    row_pieces = []
    for start in range(0, tile_rows, step_rows):
        counts_part = tile_counts[start : start + step_rows]
        vectors_part = row_block[:, start : start + step_rows]
        scores = lax.dot_general(
            vectors_part, col_block, (((0,), (0,)), ((), ())), precision=highest
        )
        baseline = col_base - row_logs[start : start + step_rows][:, None]
        positive = counts_part > 0
        pmi_target = jnp.log(jnp.where(positive, counts_part, 1.0)) + baseline
        confidence = 0.1 + 0.25 * jnp.sqrt(counts_part)
        loss_grad = (
            jnp.where(
                positive, confidence * (scores - pmi_target), jax.nn.sigmoid(scores - baseline)
            )
            * loss_scale
        )
        row_pieces.append(
            lax.dot_general(col_block, loss_grad, (((1,), (1,)), ((), ())), precision=highest)
        )
        col_term = col_term + jnp.dot(vectors_part, loss_grad, precision=highest)
    row_term = jnp.concatenate(row_pieces, axis=1)
    row_share = lax.psum_scatter(row_term, "col", scatter_dimension=1, tiled=True)
    col_share = lax.psum_scatter(col_term, "row", scatter_dimension=1, tiled=True)
    new_row_acc = row_acc + row_share * row_share
    new_col_acc = col_acc + col_share * col_share
    new_row_emb = row_emb - LEARNING_RATE * row_share / jnp.sqrt(new_row_acc)
    new_col_emb = col_emb - LEARNING_RATE * col_share / jnp.sqrt(new_col_acc)
    return (new_row_emb, new_col_emb, new_row_acc, new_col_acc)


def solution(mesh):
    return jax.shard_map(
        per_device,
        mesh=mesh,
        in_specs=(
            P("row", "col", None, None, None, None, None),
            P("row", "col", None, None, None),
            P("row", "col", None, None),
            P(None, ("row", "col")),
            P(None, ("col", "row")),
            P(None, ("row", "col")),
            P(None, ("col", "row")),
        ),
        out_specs=(
            P(None, ("row", "col")),
            P(None, ("col", "row")),
            P(None, ("row", "col")),
            P(None, ("col", "row")),
        ),
        check_vma=False,
    )
```

profile of v0, /device:TPU:2, one launch (start us, length us, event | category | flops | bytes accessed | tf_op | source)
XLA Modules:
  0.0 581.3 jit_solution(6106549809527180893)
XLA Ops:
  7.2 0.0 all-gather.3.cloned.1.call-start
  7.2 0.7 all-gather.3.cloned.1.call-update
  7.9 0.0 all-gather.5.cloned.1.call-start
  7.9 0.7 all-gather.5.cloned.1.call-update
  8.7 0.0 copy-start.9
  8.7 0.0 copy-start.8
  8.7 1.8 copy.27
  10.5 33.1 %all_to_all.10 = f32[8,32,2,8,128]{4,3,2,0,1:T(8,128)S(1)} all-to-all(f32[8,32,2,8,128]{4,3,2,0,1:T(8,128)S(1)} %bitcast.54), channel_id=1, replica_groups=mesh['row'=32,'col'=8] {'row'}, dimensions={1} | all-to-all | bytes 4194304 | tf_op jit(solution)/shard_map/all_to_all | solution.py:15
  43.6 1.5 copy.19
  45.1 8.5 %all-to-all-start.1 = ((f32[8,32,2,8,128]{4,3,2,1,0:T(8,128)}), f32[8,32,2,8,128]{4,3,2,1,0:T(8,128)S(1)}, u32[]{:S(2)}, u32[]{:S(2)}) async-start(f32[8,32,2,8,128]{4,3,2,1,0:T(8,128)} %copy.19), calls=%async_computation.1 | async-start | bytes 4194304 | tf_op jit(solution)/shard_map/all_to_all | solution.py:14
  53.6 0.0 reduce-scatter.3.cloned.1.call-start
  53.6 0.0 copy-done.9
  53.7 0.1 iota_compare_fusion
  53.8 0.1 lt.23
  53.9 0.0 copy-done.8
  53.9 0.1 copy.17
  54.1 0.1 squeeze.6
  54.2 51.8 %all-to-all-done.1 = f32[8,32,2,8,128]{4,3,2,1,0:T(8,128)S(1)} async-done(((f32[8,32,2,8,128]{4,3,2,1,0:T(8,128)}), f32[8,32,2,8,128]{4,3,2,1,0:T(8,128)S(1)}, u32[]{:S(2)}, u32[]{:S(2)}) %all-to-all-start.1) | async-done | bytes 2097184 | tf_op jit(solution)/shard_map/all_to_all | solution.py:14
  106.0 11.9 %scatter_custom_fusion = f32[4097,1024]{1,0:T(8,128)} fusion(s32[512]{0:T(512)S(1)} %bitcast.58, f32[]{:T(128)} %constant.7.clone.1, f32[64,8,8,128]{3,2,1,0:T(8,128)S(1)} %bitcast.55), kind=kCustom, calls=%fused_computation.12 | custom fusion | flops 524288 | bytes 18878468 | tf_op jit(solution)/shard_map/scatter-add | solution.py:33
  117.9 13.3 %slice_reduce_fusion = (f32[]{:T(128)}, f32[512,8,8,128]{3,1,2,0:T(8,128)}) fusion(f32[4097,1024]{1,0:T(8,128)} %scatter_custom_fusion), kind=kLoop, calls=%fused_computation.2 | loop fusion | flops 4194303 | bytes 33554436 | tf_op jit(solution)/shard_map/reduce_sum | solution.py:45
  131.2 72.8 %psum.21 = f32[]{:T(128)} all-reduce(f32[]{:T(128)} %get-tuple-element.10), channel_id=1, replica_groups=mesh['row'=32,'col'=8] {'row','col'}, use_global_device_ids=true, to_apply=%region_2.3 | all-reduce | flops 1 | bytes 8 | tf_op jit(solution)/shard_map/psum | solution.py:45
  204.7 14.3 %copy.21 = f32[512,8,8,128]{3,2,1,0:T(8,128)} copy(f32[512,8,8,128]{3,1,2,0:T(8,128)} %get-tuple-element.11) | data formatting | bytes 33554432
  218.9 7.2 %fusion.27 = (f32[32,128]{1,0:T(8,128)S(1)}, f32[128,8]{1,0:T(8,128)S(1)}) fusion(f32[128,32,8,128]{3,2,1,0:T(8,128)} %bitcast.52), kind=kLoop, calls=%fused_computation.53 | loop fusion | flops 8383488 | bytes 16797696 | tf_op jit(solution)/shard_map/reduce_sum | solution.py:42
  226.1 0.1 reduce_sum.35
  226.2 16.2 %psum.23 = f32[1024]{0:T(1024)S(1)} all-reduce(f32[1024]{0:T(1024)S(1)} %reduce_sum.35), channel_id=1, replica_groups=mesh['row'=32,'col'=8] {'col'}, use_global_device_ids=true, to_apply=%region_6.7 | all-reduce | flops 1024 | bytes 8192 | tf_op jit(solution)/shard_map/psum | solution.py:44
  242.5 107.5 %psum.22 = f32[4096]{0:T(1024)S(1)} all-reduce(f32[4096]{0:T(1024)S(1)} %bitcast.56), channel_id=1, replica_groups=mesh['row'=32,'col'=8] {'row'}, use_global_device_ids=true, to_apply=%region_4.5 | all-reduce | flops 4096 | bytes 32768 | tf_op jit(solution)/shard_map/psum | solution.py:43
  350.0 11.7 %bitcast_bitcast_fusion = f32[128,8,32,128]{3,1,2,0:T(8,128)} fusion(f32[128,32,8,128]{3,2,1,0:T(8,128)} %bitcast.53), kind=kLoop, calls=%fused_computation.1 | loop fusion | bytes 33554432 | tf_op jit(solution)/shard_map/transpose | solution.py:38
  361.7 21.9 %fusion.5 = f32[512,4096]{1,0:T(8,128)S(1)} fusion(f32[128,8,32,128]{3,1,2,0:T(8,128)} %bitcast_bitcast_fusion, f32[512]{0:T(512)S(1)} %get-tuple-element.13, f32[4096]{0:T(1024)S(1)} %log_subtract_fusion, f32[300,4096]{1,0:T(8,128)} %all-gather.5.cloned.1.call-done, f32[300,1024]{1,0:T(8,128)} %all-gather.3.cloned.1.call-done), kind=kOutput, calls=%fused_computation.17 | convolution fusion | flops 7579107328 | bytes 22398976 | tf_op jit(solution)/shard_map/dot_general | solution.py:59
  383.6 0.0 copy-start
  383.6 0.0 copy-done.2
  383.6 25.7 %fusion.3 = f32[512,4096]{1,0:T(8,128)S(1)} fusion(f32[128,8,32,128]{3,1,2,0:T(8,128)} %bitcast_bitcast_fusion, f32[512]{0:T(512)S(1)} %get-tuple-element.12, f32[4096]{0:T(1024)S(1)} %log_subtract_fusion, f32[300,4096]{1,0:T(8,128)S(1)} %copy-done.2, f32[300,1024]{1,0:T(8,128)S(1)} %copy-done.3), kind=kOutput, calls=%fused_computation.15 | convolution fusion | flops 7579107328 | bytes 22398976 | tf_op jit(solution)/shard_map/dot_general | solution.py:59
  409.3 0.0 copy-start.1
  409.3 8.6 %convolution_bitcast_fusion.1 = f32[300,512]{1,0:T(8,128)S(1)} fusion(f32[512,4096]{1,0:T(8,128)S(1)} %fusion.3, f32[300,4096]{1,0:T(8,128)S(1)} %copy-done.2), kind=kOutput, calls=%fused_computation.38 | convolution fusion | flops 7549747200 | bytes 13918208 | tf_op jit(solution)/shard_map/dot_general | solution.py:73
  417.9 8.8 %convolution_bitcast_fusion = f32[300,512]{1,0:T(8,128)S(1)} fusion(f32[512,4096]{1,0:T(8,128)S(1)} %fusion.5, f32[300,4096]{1,0:T(8,128)S(1)} %copy-done.2), kind=kOutput, calls=%fused_computation.37 | convolution fusion | flops 7549747200 | bytes 13918208 | tf_op jit(solution)/shard_map/dot_general | solution.py:73
  426.7 1.1 pad_maximum_fusion
  427.9 0.0 reduce-scatter.3.cloned.1.call-update
  427.9 0.0 reduce-scatter.5.cloned.1.call-start
  428.0 11.3 %fusion.23 = f32[4096,300]{0,1:T(8,128)S(1)} fusion(f32[512,4096]{1,0:T(8,128)} %copy-done.1, f32[300,1024]{1,0:T(8,128)S(1)} %copy-done.3), kind=kOutput, calls=%fused_computation.42 | convolution fusion | flops 7549747200 | bytes 13926400 | tf_op jit(solution)/shard_map/dot_general | solution.py:75
  439.2 0.0 copy-start.4
  439.2 0.0 copy-start.6
  439.2 0.0 copy-start.5
  439.3 0.0 copy-start.7
  439.3 12.8 %fusion.18 = f32[300,4096]{1,0:T(8,128)} fusion(f32[4096,300]{0,1:T(8,128)S(1)} %fusion.23, f32[512,4096]{1,0:T(8,128)} %copy-done, f32[300,1024]{1,0:T(8,128)S(1)} %copy-done.3), kind=kOutput, calls=%fused_computation.33 | convolution fusion | flops 7550976000 | bytes 18907136 | tf_op jit(solution)/shard_map/dot_general | solution.py:75
  452.1 0.0 reduce-scatter.5.cloned.1.call-update
  452.1 25.8 %reduce-scatter.3.cloned.1.call-done = f32[300,128]{1,0:T(8,128)} async-done(((f32[300,1024]{1,0:T(8,128)}), f32[300,128]{1,0:T(8,128)}) %reduce-scatter.3.cloned.1.call-update) | async-done | bytes 153616 | tf_op jit(solution)/shard_map/reduce_scatter | solution.py:77
  477.9 1.7 multiply_subtract_fusion.1
  479.6 93.4 %reduce-scatter.5.cloned.1.call-done = f32[300,128]{1,0:T(8,128)} async-done(((f32[300,4096]{1,0:T(8,128)}), f32[300,128]{1,0:T(8,128)}) %reduce-scatter.5.cloned.1.call-update) | async-done | bytes 153616 | tf_op jit(solution)/shard_map/reduce_scatter | solution.py:78
  572.9 1.7 multiply_subtract_fusion
  (15 shorter events, 0.0 us)
Async XLA Ops:
  7.2 354.5 %all-gather.3.cloned.1.call-start = ((), (), s32[]{:S(2)}) async-start(), calls=%async_computation.4 | async-start | bytes 1400832 | tf_op jit(solution)/shard_map/all_gather | solution.py:46
  7.9 353.7 %all-gather.5.cloned.1.call-start = ((), (), s32[]{:S(2)}) async-start(), calls=%async_computation.5 | async-start | bytes 5136384 | tf_op jit(solution)/shard_map/all_gather | solution.py:47
  8.7 45.0 %copy-start.9 = (s32[1,1,8,32]{3,2,1,0:T(8,128)S(1)}, s32[1,1,8,32]{3,2,1,0:T(8,128)}, u32[]{:S(2)}) copy-start(s32[1,1,8,32]{3,2,1,0:T(8,128)} %param.9) | copy-start | bytes 3076
  8.7 45.3 %copy-start.8 = (s32[1,1,8,32,2]{3,4,2,1,0:T(2,128)S(1)}, s32[1,1,8,32,2]{3,4,2,1,0:T(2,128)}, u32[]{:S(2)}) copy-start(s32[1,1,8,32,2]{3,4,2,1,0:T(2,128)} %param.8) | copy-start | bytes 6148
  45.1 60.9 %all-to-all-start.1 = ((f32[8,32,2,8,128]{4,3,2,1,0:T(8,128)}), f32[8,32,2,8,128]{4,3,2,1,0:T(8,128)S(1)}, u32[]{:S(2)}, u32[]{:S(2)}) async-start(f32[8,32,2,8,128]{4,3,2,1,0:T(8,128)} %copy.19), calls=%async_computation.1 | async-start | bytes 4194304 | tf_op jit(solution)/shard_map/all_to_all | solution.py:14
  53.6 424.3 %reduce-scatter.3.cloned.1.call-start = ((), (), s32[]{:S(2)}) async-start(), calls=%async_computation.6 | async-start | bytes 1400832 | tf_op jit(solution)/shard_map/reduce_scatter | solution.py:77
  361.6 22.0 %copy-start.2 = (f32[300,4096]{1,0:T(8,128)S(1)}, f32[300,4096]{1,0:T(8,128)}, u32[]{:S(2)}) copy-start(f32[300,4096]{1,0:T(8,128)} %all-gather.5.cloned.1.call-done) | copy-start | bytes 14745604
  361.6 22.0 %copy-start.3 = (f32[300,1024]{1,0:T(8,128)S(1)}, f32[300,1024]{1,0:T(8,128)}, u32[]{:S(2)}) copy-start(f32[300,1024]{1,0:T(8,128)} %all-gather.3.cloned.1.call-done) | copy-start | bytes 3686404
  383.6 34.3 %copy-start = (f32[512,4096]{1,0:T(8,128)}, f32[512,4096]{1,0:T(8,128)S(1)}, u32[]{:S(2)}) copy-start(f32[512,4096]{1,0:T(8,128)S(1)} %fusion.5) | copy-start | bytes 25165828
  409.3 8.6 %copy-start.1 = (f32[512,4096]{1,0:T(8,128)}, f32[512,4096]{1,0:T(8,128)S(1)}, u32[]{:S(2)}) copy-start(f32[512,4096]{1,0:T(8,128)S(1)} %fusion.3) | copy-start | bytes 25165828
  427.9 145.0 %reduce-scatter.5.cloned.1.call-start = ((), (), s32[]{:S(2)}) async-start(), calls=%async_computation.7 | async-start | bytes 5136384 | tf_op jit(solution)/shard_map/reduce_scatter | solution.py:78
  439.2 38.7 %copy-start.4 = (f32[300,128]{1,0:T(8,128)S(1)}, f32[300,128]{1,0:T(8,128)}, u32[]{:S(2)}) copy-start(f32[300,128]{1,0:T(8,128)} %param.10) | copy-start | bytes 460804
  439.2 38.7 %copy-start.6 = (f32[300,128]{1,0:T(8,128)S(1)}, f32[300,128]{1,0:T(8,128)}, u32[]{:S(2)}) copy-start(f32[300,128]{1,0:T(8,128)} %param.12) | copy-start | bytes 460804
  439.2 133.7 %copy-start.5 = (f32[300,128]{1,0:T(8,128)S(1)}, f32[300,128]{1,0:T(8,128)}, u32[]{:S(2)}) copy-start(f32[300,128]{1,0:T(8,128)} %param.11) | copy-start | bytes 460804
  439.3 133.7 %copy-start.7 = (f32[300,128]{1,0:T(8,128)S(1)}, f32[300,128]{1,0:T(8,128)}, u32[]{:S(2)}) copy-start(f32[300,128]{1,0:T(8,128)} %param.13) | copy-start | bytes 460804
Sparse Core Ops, SparseCore 0:
  9.7 44.0 all-gather.2
  56.2 54.9 all-gather.4
  428.0 49.8 reduce-scatter.2
  481.9 91.0 reduce-scatter.4
where the time goes:
time: 589 us; the launch traced here: 581 us
  blocking collectives  230 us (39%)
  waiting for transfers between devices  172 us (29%)
  matrix products  89 us (15%)
  other arithmetic  37 us (6%)
  local copies, waits for them, and re-layouts  29.9 us (5%)
  between operations  14.8 us (3%)
  starting transfers between devices  8.62 us (1%)
    psum x1, blocking collectives, per_device(): col_mass = lax.psum(col_part, 'row')  107 us
    reduce_scatter x1, waiting for transfers between devices, per_device(): lax.psum_scatter(col_term, 'row', scatter_dimension=1, tiled=True)  93.4 us
    psum x1, blocking collectives, per_device(): grand_total = lax.psum(jnp.sum(row_part), ('row', 'col'))  72.8 us
    all_to_all x1, waiting for transfers between devices, per_device(): lax.all_to_all(lax.all_to_all(outgoing, 'row', split_axis=1, concat_axis=...  51.8 us
    dot_general x2, matrix products, per_device(): lax.dot_general(vectors_part, col_block, (((0,), (0,)), ((), ())), precis...  47.6 us
    all_to_all x1, blocking collectives, per_device(): lax.all_to_all(outgoing, 'row', split_axis=1, concat_axis=1, tiled=True)  33.1 us
    reduce_scatter x1, waiting for transfers between devices, per_device(): lax.psum_scatter(row_term, 'col', scatter_dimension=1, tiled=True)  25.8 us
    dot_general x2, matrix products, per_device(): col_term = col_term + jnp.dot(vectors_part, loss_grad, precision=highest)  24.1 us
  transfers between devices with their start and end apart: 5, of which 3 were waited for; matrix products, arithmetic and copies ran while one was open for 15% of the time, Pallas kernels for 0%

commit v1 on v0

--- a/solution.py
+++ b/solution.py
@@ -4,6 +4,11 @@
 from jax.sharding import PartitionSpec as P
 
 LEARNING_RATE = 0.2
+
+
+def add_all(x, name):
+    shards = lax.all_gather(x, name)
+    return jnp.sum(shards, axis=0)
 
 
 def per_device(blocks, plan, live, row_emb, col_emb, row_acc, col_acc):
@@ -40,7 +45,7 @@
     )
     row_part = jnp.sum(tile_counts, axis=1)
     col_part = jnp.sum(tile_counts, axis=0)
-    col_mass = lax.psum(col_part, "row")
+    col_mass = add_all(col_part, "row")
     row_mass = lax.psum(row_part, "col")
     grand_total = lax.psum(jnp.sum(row_part), ("row", "col"))
     row_block = lax.all_gather(row_emb, "col", axis=1, tiled=True)

time: 589 us -> 491 us (0.83)
  blocking collectives: 230 us -> 146 us
  waiting for transfers between devices: 172 us -> 158 us
    psum x1 -> x0, blocking collectives: 107 us -> none  [per_device(): col_mass = lax.psum(col_part, 'row')]
    all_gather x0 -> x1, blocking collectives: none -> 23.7 us  [add_all(): shards = lax.all_gather(x, name)]
    reduce_scatter x1, waiting for transfers between devices: 25.8 us -> 11.2 us  [per_device(): lax.psum_scatter(row_term, 'col', scatter_dimension=1, tiled=True)]
  transfers between devices with their start and end apart: 5 -> 5, of which waited for: 3 -> 3; matrix products, arithmetic and copies ran while one was open for 15% -> 18% of each run, Pallas kernels for 0% -> 0%
where the time goes in v1:
time: 491 us; the launch traced here: 483 us
  waiting for transfers between devices  158 us (32%)
  blocking collectives  146 us (30%)
  matrix products  89.1 us (18%)
  other arithmetic  37.4 us (8%)
  local copies, waits for them, and re-layouts  29.9 us (6%)
  between operations  14.9 us (3%)
  starting transfers between devices  8.62 us (2%)
    reduce_scatter x1, waiting for transfers between devices, per_device(): lax.psum_scatter(col_term, 'row', scatter_dimension=1, tiled=True)  93.3 us
    psum x1, blocking collectives, per_device(): grand_total = lax.psum(jnp.sum(row_part), ('row', 'col'))  72.8 us
    all_to_all x1, waiting for transfers between devices, per_device(): lax.all_to_all(lax.all_to_all(outgoing, 'row', split_axis=1, concat_axis=...  51.8 us
    dot_general x2, matrix products, per_device(): lax.dot_general(vectors_part, col_block, (((0,), (0,)), ((), ())), precis...  47.6 us
    all_to_all x1, blocking collectives, per_device(): lax.all_to_all(outgoing, 'row', split_axis=1, concat_axis=1, tiled=True)  33.1 us
    dot_general x2, matrix products, per_device(): col_term = col_term + jnp.dot(vectors_part, loss_grad, precision=highest)  24.1 us
    all_gather x1, blocking collectives, add_all(): shards = lax.all_gather(x, name)  23.7 us
    dot_general x2, matrix products, per_device(): lax.dot_general(col_block, loss_grad, (((1,), (1,)), ((), ())), precision...  17.4 us
  transfers between devices with their start and end apart: 5, of which 3 were waited for; matrix products, arithmetic and copies ran while one was open for 18% of the time, Pallas kernels for 0%

profile of v1, /device:TPU:2, one launch (start us, length us, event | category | flops | bytes accessed | tf_op | source)
XLA Modules:
  0.0 483.2 jit_solution(10882340301369968032)
XLA Ops:
  7.2 0.0 all-gather.4.cloned.1.call-start
  7.2 0.7 all-gather.4.cloned.1.call-update
  7.9 0.0 all-gather.6.cloned.1.call-start
  7.9 0.7 all-gather.6.cloned.1.call-update
  8.7 0.0 copy-start.9
  8.7 1.8 copy.27
  10.5 33.1 %all_to_all.10 = f32[8,32,2,8,128]{4,3,2,0,1:T(8,128)S(1)} all-to-all(f32[8,32,2,8,128]{4,3,2,0,1:T(8,128)S(1)} %bitcast.54), channel_id=1, replica_groups=mesh['row'=32,'col'=8] {'row'}, dimensions={1} | all-to-all | bytes 4194304 | tf_op jit(solution)/shard_map/all_to_all | solution.py:20
  43.6 1.5 copy.19
  45.1 8.5 %all-to-all-start.1 = ((f32[8,32,2,8,128]{4,3,2,1,0:T(8,128)}), f32[8,32,2,8,128]{4,3,2,1,0:T(8,128)S(1)}, u32[]{:S(2)}, u32[]{:S(2)}) async-start(f32[8,32,2,8,128]{4,3,2,1,0:T(8,128)} %copy.19), calls=%async_computation.1 | async-start | bytes 4194304 | tf_op jit(solution)/shard_map/all_to_all | solution.py:19
  53.6 0.0 reduce-scatter.3.cloned.1.call-start
  53.7 0.1 iota_compare_fusion
  53.8 0.1 lt.23
  53.9 0.1 copy.17
  54.1 0.1 squeeze.6
  54.2 51.8 %all-to-all-done.1 = f32[8,32,2,8,128]{4,3,2,1,0:T(8,128)S(1)} async-done(((f32[8,32,2,8,128]{4,3,2,1,0:T(8,128)}), f32[8,32,2,8,128]{4,3,2,1,0:T(8,128)S(1)}, u32[]{:S(2)}, u32[]{:S(2)}) %all-to-all-start.1) | async-done | bytes 2097184 | tf_op jit(solution)/shard_map/all_to_all | solution.py:19
  106.0 11.9 %scatter_custom_fusion = f32[4097,1024]{1,0:T(8,128)} fusion(s32[512]{0:T(512)S(1)} %bitcast.58, f32[]{:T(128)} %constant.7.clone.1, f32[64,8,8,128]{3,2,1,0:T(8,128)S(1)} %bitcast.55), kind=kCustom, calls=%fused_computation.12 | custom fusion | flops 524288 | bytes 18878468 | tf_op jit(solution)/shard_map/scatter-add | solution.py:38
  117.9 13.3 %slice_reduce_fusion = (f32[]{:T(128)}, f32[512,8,8,128]{3,1,2,0:T(8,128)}) fusion(f32[4097,1024]{1,0:T(8,128)} %scatter_custom_fusion), kind=kLoop, calls=%fused_computation.2 | loop fusion | flops 4194303 | bytes 33554436 | tf_op jit(solution)/shard_map/reduce_sum | solution.py:50
  131.2 72.8 %psum.14 = f32[]{:T(128)} all-reduce(f32[]{:T(128)} %get-tuple-element.10), channel_id=1, replica_groups=mesh['row'=32,'col'=8] {'row','col'}, use_global_device_ids=true, to_apply=%region_2.3 | all-reduce | flops 1 | bytes 8 | tf_op jit(solution)/shard_map/psum | solution.py:50
  204.7 14.3 %copy.21 = f32[512,8,8,128]{3,2,1,0:T(8,128)} copy(f32[512,8,8,128]{3,1,2,0:T(8,128)} %get-tuple-element.11) | data formatting | bytes 33554432
  218.9 7.2 %fusion.27 = (f32[32,128]{1,0:T(8,128)S(1)}, f32[128,8]{1,0:T(8,128)S(1)}) fusion(f32[128,32,8,128]{3,2,1,0:T(8,128)} %bitcast.52), kind=kLoop, calls=%fused_computation.53 | loop fusion | flops 8383488 | bytes 16797696 | tf_op jit(solution)/shard_map/reduce_sum | solution.py:47
  226.1 0.1 reduce_sum.42
  226.2 16.2 %psum.15 = f32[1024]{0:T(1024)S(1)} all-reduce(f32[1024]{0:T(1024)S(1)} %reduce_sum.42), channel_id=1, replica_groups=mesh['row'=32,'col'=8] {'col'}, use_global_device_ids=true, to_apply=%region_6.7 | all-reduce | flops 1024 | bytes 8192 | tf_op jit(solution)/shard_map/psum | solution.py:49
  242.5 23.7 %all-gather = f32[32,1,4096]{2,1,0:T(1,128)S(1)} all-gather(f32[1,1,4096]{2,1,0:T(1,128)S(1)} %bitcast.56), channel_id=1, replica_groups=mesh['row'=32,'col'=8] {'row'}, dimensions={0}, use_global_device_ids=true | all-gather | bytes 540672 | tf_op jit(solution)/shard_map/all_gather | solution.py:10
  266.1 0.4 reduce_sum.40
  266.5 11.7 %bitcast_bitcast_fusion = f32[128,8,32,128]{3,1,2,0:T(8,128)} fusion(f32[128,32,8,128]{3,2,1,0:T(8,128)} %bitcast.53), kind=kLoop, calls=%fused_computation.1 | loop fusion | bytes 33554432 | tf_op jit(solution)/shard_map/transpose | solution.py:43
  278.2 21.9 %fusion.5 = f32[512,4096]{1,0:T(8,128)S(1)} fusion(f32[128,8,32,128]{3,1,2,0:T(8,128)} %bitcast_bitcast_fusion, f32[512]{0:T(512)S(1)} %get-tuple-element.13, f32[4096]{0:T(1024)S(1)} %log_subtract_fusion, f32[300,4096]{1,0:T(8,128)} %all-gather.6.cloned.1.call-done, f32[300,1024]{1,0:T(8,128)} %all-gather.4.cloned.1.call-done), kind=kOutput, calls=%fused_computation.17 | convolution fusion | flops 7579107328 | bytes 22398976 | tf_op jit(solution)/shard_map/dot_general | solution.py:64
  300.1 0.0 copy-start
  300.2 0.0 copy-done.2
  300.2 0.0 copy-done.3
  300.2 25.7 %fusion.3 = f32[512,4096]{1,0:T(8,128)S(1)} fusion(f32[128,8,32,128]{3,1,2,0:T(8,128)} %bitcast_bitcast_fusion, f32[512]{0:T(512)S(1)} %get-tuple-element.12, f32[4096]{0:T(1024)S(1)} %log_subtract_fusion, f32[300,4096]{1,0:T(8,128)S(1)} %copy-done.2, f32[300,1024]{1,0:T(8,128)S(1)} %copy-done.3), kind=kOutput, calls=%fused_computation.15 | convolution fusion | flops 7579107328 | bytes 22398976 | tf_op jit(solution)/shard_map/dot_general | solution.py:64
  325.9 8.6 %convolution_bitcast_fusion.1 = f32[300,512]{1,0:T(8,128)S(1)} fusion(f32[512,4096]{1,0:T(8,128)S(1)} %fusion.3, f32[300,4096]{1,0:T(8,128)S(1)} %copy-done.2), kind=kOutput, calls=%fused_computation.38 | convolution fusion | flops 7549747200 | bytes 13918208 | tf_op jit(solution)/shard_map/dot_general | solution.py:78
  334.5 0.0 copy-done
  334.5 0.0 copy-done.1
  334.5 8.8 %convolution_bitcast_fusion = f32[300,512]{1,0:T(8,128)S(1)} fusion(f32[512,4096]{1,0:T(8,128)S(1)} %fusion.5, f32[300,4096]{1,0:T(8,128)S(1)} %copy-done.2), kind=kOutput, calls=%fused_computation.37 | convolution fusion | flops 7549747200 | bytes 13918208 | tf_op jit(solution)/shard_map/dot_general | solution.py:78
  343.3 1.1 pad_maximum_fusion
  344.4 0.0 reduce-scatter.3.cloned.1.call-update
  344.5 0.0 reduce-scatter.5.cloned.1.call-start
  344.5 11.3 %fusion.23 = f32[4096,300]{0,1:T(8,128)S(1)} fusion(f32[512,4096]{1,0:T(8,128)} %copy-done.1, f32[300,1024]{1,0:T(8,128)S(1)} %copy-done.3), kind=kOutput, calls=%fused_computation.42 | convolution fusion | flops 7549747200 | bytes 13926400 | tf_op jit(solution)/shard_map/dot_general | solution.py:80
  355.8 0.0 copy-start.4
  355.8 0.0 copy-start.6
  355.8 0.0 copy-start.5
  355.8 0.0 copy-start.7
  355.8 12.8 %fusion.18 = f32[300,4096]{1,0:T(8,128)} fusion(f32[4096,300]{0,1:T(8,128)S(1)} %fusion.23, f32[512,4096]{1,0:T(8,128)} %copy-done, f32[300,1024]{1,0:T(8,128)S(1)} %copy-done.3), kind=kOutput, calls=%fused_computation.33 | convolution fusion | flops 7550976000 | bytes 18907136 | tf_op jit(solution)/shard_map/dot_general | solution.py:80
  368.6 0.0 reduce-scatter.5.cloned.1.call-update
  368.6 11.2 %reduce-scatter.3.cloned.1.call-done = f32[300,128]{1,0:T(8,128)} async-done(((f32[300,1024]{1,0:T(8,128)}), f32[300,128]{1,0:T(8,128)}) %reduce-scatter.3.cloned.1.call-update) | async-done | bytes 153616 | tf_op jit(solution)/shard_map/reduce_scatter | solution.py:82
  379.9 1.7 multiply_subtract_fusion.1
  381.5 93.3 %reduce-scatter.5.cloned.1.call-done = f32[300,128]{1,0:T(8,128)} async-done(((f32[300,4096]{1,0:T(8,128)}), f32[300,128]{1,0:T(8,128)}) %reduce-scatter.5.cloned.1.call-update) | async-done | bytes 153616 | tf_op jit(solution)/shard_map/reduce_scatter | solution.py:83
  474.9 1.7 multiply_subtract_fusion
  (16 shorter events, 0.1 us)
Async XLA Ops:
  7.2 271.0 %all-gather.4.cloned.1.call-start = ((), (), s32[]{:S(2)}) async-start(), calls=%async_computation.4 | async-start | bytes 1400832 | tf_op jit(solution)/shard_map/all_gather | solution.py:51
  7.9 270.3 %all-gather.6.cloned.1.call-start = ((), (), s32[]{:S(2)}) async-start(), calls=%async_computation.5 | async-start | bytes 5136384 | tf_op jit(solution)/shard_map/all_gather | solution.py:52
  8.7 45.0 %copy-start.9 = (s32[1,1,8,32]{3,2,1,0:T(8,128)S(1)}, s32[1,1,8,32]{3,2,1,0:T(8,128)}, u32[]{:S(2)}) copy-start(s32[1,1,8,32]{3,2,1,0:T(8,128)} %param.9) | copy-start | bytes 3076
  8.7 45.3 %copy-start.8 = (s32[1,1,8,32,2]{3,4,2,1,0:T(2,128)S(1)}, s32[1,1,8,32,2]{3,4,2,1,0:T(2,128)}, u32[]{:S(2)}) copy-start(s32[1,1,8,32,2]{3,4,2,1,0:T(2,128)} %param.8) | copy-start | bytes 6148
  45.1 60.9 %all-to-all-start.1 = ((f32[8,32,2,8,128]{4,3,2,1,0:T(8,128)}), f32[8,32,2,8,128]{4,3,2,1,0:T(8,128)S(1)}, u32[]{:S(2)}, u32[]{:S(2)}) async-start(f32[8,32,2,8,128]{4,3,2,1,0:T(8,128)} %copy.19), calls=%async_computation.1 | async-start | bytes 4194304 | tf_op jit(solution)/shard_map/all_to_all | solution.py:19
  53.6 326.3 %reduce-scatter.3.cloned.1.call-start = ((), (), s32[]{:S(2)}) async-start(), calls=%async_computation.6 | async-start | bytes 1400832 | tf_op jit(solution)/shard_map/reduce_scatter | solution.py:82
  278.2 22.0 %copy-start.2 = (f32[300,4096]{1,0:T(8,128)S(1)}, f32[300,4096]{1,0:T(8,128)}, u32[]{:S(2)}) copy-start(f32[300,4096]{1,0:T(8,128)} %all-gather.6.cloned.1.call-done) | copy-start | bytes 14745604
  278.2 22.0 %copy-start.3 = (f32[300,1024]{1,0:T(8,128)S(1)}, f32[300,1024]{1,0:T(8,128)}, u32[]{:S(2)}) copy-start(f32[300,1024]{1,0:T(8,128)} %all-gather.4.cloned.1.call-done) | copy-start | bytes 3686404
  300.1 34.3 %copy-start = (f32[512,4096]{1,0:T(8,128)}, f32[512,4096]{1,0:T(8,128)S(1)}, u32[]{:S(2)}) copy-start(f32[512,4096]{1,0:T(8,128)S(1)} %fusion.5) | copy-start | bytes 25165828
  325.9 8.6 %copy-start.1 = (f32[512,4096]{1,0:T(8,128)}, f32[512,4096]{1,0:T(8,128)S(1)}, u32[]{:S(2)}) copy-start(f32[512,4096]{1,0:T(8,128)S(1)} %fusion.3) | copy-start | bytes 25165828
  344.5 130.4 %reduce-scatter.5.cloned.1.call-start = ((), (), s32[]{:S(2)}) async-start(), calls=%async_computation.7 | async-start | bytes 5136384 | tf_op jit(solution)/shard_map/reduce_scatter | solution.py:83
  355.8 24.1 %copy-start.4 = (f32[300,128]{1,0:T(8,128)S(1)}, f32[300,128]{1,0:T(8,128)}, u32[]{:S(2)}) copy-start(f32[300,128]{1,0:T(8,128)} %param.10) | copy-start | bytes 460804
  355.8 24.1 %copy-start.6 = (f32[300,128]{1,0:T(8,128)S(1)}, f32[300,128]{1,0:T(8,128)}, u32[]{:S(2)}) copy-start(f32[300,128]{1,0:T(8,128)} %param.12) | copy-start | bytes 460804
  355.8 119.1 %copy-start.5 = (f32[300,128]{1,0:T(8,128)S(1)}, f32[300,128]{1,0:T(8,128)}, u32[]{:S(2)}) copy-start(f32[300,128]{1,0:T(8,128)} %param.11) | copy-start | bytes 460804
  355.8 119.1 %copy-start.7 = (f32[300,128]{1,0:T(8,128)S(1)}, f32[300,128]{1,0:T(8,128)}, u32[]{:S(2)}) copy-start(f32[300,128]{1,0:T(8,128)} %param.13) | copy-start | bytes 460804
Sparse Core Ops, SparseCore 0:
  9.7 44.0 all-gather.3
  56.2 54.9 all-gather.5
  344.6 35.2 reduce-scatter.2
  383.8 91.0 reduce-scatter.4
